TPU v7x, 32 devices: a whole 2x2x4 slice. The times are simulated.
32 devices in a mesh: tm: 4 (over z), dom: 8 (over y, x, core).
Axes of the slice: x: 2, y: 2, z: 4, core: 2. Of those that a mesh axis runs over, the one named last changes fastest.
Arguments:
- video_group: bfloat16 [2, 16, 112, 128, 128], P(None, 'tm', 'dom'), may hold values from -6 to 6
- pairing: int32 [4, 2], P('tm'), may hold values from 0 to 1, each once within a row
- weight_one: bfloat16 [3, 3, 3, 128, 128], replicated, may hold values from -0.109375 to 0.109375
- weight_down: bfloat16 [3, 3, 128, 256], replicated, may hold values from -0.1875 to 0.1875
- weight_two: bfloat16 [3, 3, 3, 256, 256], replicated, may hold values from -0.078125 to 0.078125
Outputs:
- encoded: bfloat16 [2, 16, 56, 64, 256], P(None, 'tm', 'dom')
Inputs may be any that keep to these rules, and one draw needn't show every extreme that they name: Each row of pairing names every clip slot exactly once.
All inputs are finite; a program needn't handle non-finite values.
Results may differ from a plain program's by a relative error of at most 0.008.
Values may be sent and summed in bfloat16 or wider, within the bound.
A program may use at most 128 MiB of HBM per device.

v0:
```python
import functools

import jax
import jax.numpy as jnp
from jax import lax
from jax.experimental import pallas as pl
from jax.experimental.pallas import tpu as pltpu
from jax.sharding import PartitionSpec as P

MESH = pl.DeviceIdType.MESH
F32, BF16 = jnp.float32, jnp.bfloat16


def silu(v):
    half = 0.5 * v
    return half + half * jnp.tanh(half)


def chunk_rows(rows, width, limit):
    return max(d for d in range(1, rows + 1) if rows % d == 0 and (d == 1 or d * width <= limit))


def kernel(
    n_tm, n_dom,
    video, pairing, weight_one, weight_down, weight_two, out,
    vbuf, arr0, arr1, x4, resid, w1, wd, w2, stage, stage_raw, h3, stage_h,
    red, gbuf, garr0, garr1, g3, stage_g, obuf,
    local_sem, send_sem, recv_sem,
):
    slots, frames, rows, width, ch1 = video.shape
    rows2, cols2, ch2 = rows // 2, width // 2, out.shape[-1]
    tm, dom = lax.axis_index("tm"), lax.axis_index("dom")
    arr, garr = (arr0, arr1), (garr0, garr1)
    has_prev, has_next = tm > 0, tm < n_tm - 1
    has_up, has_down = dom > 0, dom < n_dom - 1
    prev, nxt, up, down = (tm - 1, dom), (tm + 1, dom), (tm, dom - 1), (tm, dom + 1)

    loads = [
        pltpu.make_async_copy(video, vbuf.at[:, :, 1 : rows + 1], local_sem.at[0]),
        pltpu.make_async_copy(weight_one, w1.at[:, 0 : 3 * ch1, 0:ch1], local_sem.at[1]),
        pltpu.make_async_copy(weight_one, w1.at[:, ch1 : 4 * ch1, ch1 : 2 * ch1], local_sem.at[2]),
        pltpu.make_async_copy(weight_down, wd, local_sem.at[3]),
        pltpu.make_async_copy(weight_two, w2, local_sem.at[4]),
    ]
    for load in loads:
        load.start()

    barrier = pltpu.get_barrier_semaphore()
    for there, device in ((has_prev, prev), (has_next, nxt), (has_up, up), (has_down, down)):
        @pl.when(there)
        def _():
            pl.semaphore_signal(barrier, inc=1, device_id=device, device_id_type=MESH)
    peers = sum(there.astype(jnp.int32) for there in (has_prev, has_next, has_up, has_down))
    pl.semaphore_wait(barrier, peers)

    counter = [0]

    def remote(src, dst, device, sends, receives):
        index = counter[0]
        counter[0] += 1
        copy = pltpu.make_async_remote_copy(
            src_ref=src, dst_ref=dst, send_sem=send_sem.at[index], recv_sem=recv_sem.at[index],
            device_id=device, device_id_type=MESH,
        )
        sent.append((copy, sends))
        return copy, sends, receives

    sent = []

    def start(item):
        @pl.when(item[1])
        def _():
            item[0].start()

    def arrive(item):
        @pl.when(item[2])
        def _():
            item[0].wait_recv()

    frame_moves = [
        remote(video.at[:, frames - 2 + e], arr[e].at[:, 1 : rows + 1], nxt, has_next, has_prev)
        for e in (0, 1)
    ]
    own_rows = [
        remote(video.at[:, :, 0:2], vbuf.at[:, :, rows + 1 : rows + 3], up, has_up, has_down),
        remote(video.at[:, :, rows - 1 : rows], vbuf.at[:, :, 0:1], down, has_down, has_up),
    ]
    relay_up, relay_down = has_prev & has_up, has_prev & has_down
    frame_rows = [
        [
            remote(arr[e].at[:, 1:3], arr[e].at[:, rows + 1 : rows + 3], up, relay_up, relay_down),
            remote(arr[e].at[:, rows : rows + 1], arr[e].at[:, 0:1], down, relay_down, relay_up),
        ]
        for e in (0, 1)
    ]
    gated_moves = [
        remote(
            gbuf.at[frames - 2 + e, :, 1 : rows2 + 1], garr[e].at[:, 1 : rows2 + 1],
            nxt, has_next, has_prev,
        )
        for e in (0, 1)
    ]
    gated_rows = [
        [
            remote(gbuf.at[f, :, 1:2], gbuf.at[f, :, rows2 + 1 : rows2 + 2], up, has_up, has_down),
            remote(gbuf.at[f, :, rows2 : rows2 + 1], gbuf.at[f, :, 0:1], down, has_down, has_up),
        ]
        for f in range(frames)
    ]
    gated_frame_rows = [
        [
            remote(garr[e].at[:, 1:2], garr[e].at[:, rows2 + 1 : rows2 + 2], up, relay_up, relay_down),
            remote(garr[e].at[:, rows2 : rows2 + 1], garr[e].at[:, 0:1], down, relay_down, relay_up),
        ]
        for e in (0, 1)
    ]

    for item in own_rows:
        start(item)
    start(frame_moves[1])
    start(frame_moves[0])

    w1[:, 3 * ch1 : 4 * ch1, 0:ch1] = jnp.zeros((w1.shape[0], ch1, ch1), BF16)
    w1[:, 0:ch1, ch1 : 2 * ch1] = jnp.zeros((w1.shape[0], ch1, ch1), BF16)
    stage[:, 0:8] = jnp.zeros((rows + 3, 8, ch1), F32)
    stage[:, width + 8 : width + 16] = jnp.zeros((rows + 3, 8, ch1), F32)
    stage_h[:, cols2 : cols2 + 8] = jnp.zeros((stage_h.shape[0], 8, ch1), F32)
    stage_g[:, 0:8] = jnp.zeros((rows2 + 2, 8, ch2), F32)
    stage_g[:, cols2 + 8 : cols2 + 16] = jnp.zeros((rows2 + 2, 8, ch2), F32)

    @pl.when(jnp.logical_not(has_up))
    def _():
        vbuf[:, :, 0:1] = jnp.zeros((slots, frames, 1, width, ch1), BF16)
        gbuf[:, :, 0:1] = jnp.zeros((frames, slots, 1, cols2, ch2), BF16)
        for e in (0, 1):
            arr[e][:, 0:1] = jnp.zeros((slots, 1, width, ch1), BF16)
            garr[e][:, 0:1] = jnp.zeros((slots, 1, cols2, ch2), BF16)

    @pl.when(jnp.logical_not(has_down))
    def _():
        vbuf[:, :, rows + 1 : rows + 3] = jnp.zeros((slots, frames, 2, width, ch1), BF16)
        gbuf[:, :, rows2 + 1 : rows2 + 2] = jnp.zeros((frames, slots, 1, cols2, ch2), BF16)
        for e in (0, 1):
            arr[e][:, rows + 1 : rows + 3] = jnp.zeros((slots, 2, width, ch1), BF16)
            garr[e][:, rows2 + 1 : rows2 + 2] = jnp.zeros((slots, 1, cols2, ch2), BF16)

    def spread_activated(source, s, e):
        def one(r, carry):
            v = source(r).astype(F32)
            stage[r, 8 : width + 8] = silu(v)
            for c in range(4):
                part = stage[r, pl.ds(7 + c, cols2, stride=2), :]
                x4[s, e, r, :, c * ch1 : (c + 1) * ch1] = part.astype(BF16)
            return carry

        lax.fori_loop(0, rows + 3, one, 0, unroll=2)

    def spread_own(f):
        def slot(s, carry):
            spread_activated(lambda r: vbuf[s, f, r], s, f + 2)

            def one(r, inner):
                stage_raw[r] = vbuf[s, f, r + 1].astype(F32)
                for c in range(2):
                    part = stage_raw[r, pl.ds(c, cols2, stride=2), :]
                    resid[s, f, r, :, c * ch1 : (c + 1) * ch1] = part.astype(BF16)
                return inner

            lax.fori_loop(0, rows + 1, one, 0, unroll=2)
            return carry

        lax.fori_loop(0, slots, slot, 0)

    def spread_arrived(e):
        @pl.when(has_prev)
        def _():
            def slot(s, carry):
                source_slot = pairing[0, s]
                spread_activated(lambda r: arr[e][source_slot, r], s, e)
                return carry

            lax.fori_loop(0, slots, slot, 0)

        @pl.when(jnp.logical_not(has_prev))
        def _():
            x4[:, e] = jnp.zeros((slots, rows + 3, cols2, 4 * ch1), BF16)

    step = chunk_rows(rows + 1, cols2, 512)
    chunks = (rows + 1) // step

    def first_section(f):
        def slot(s, carry):
            def chunk(i, inner):
                first = i * step
                taps = [
                    x4[s, f + kf, pl.ds(first + kr, step)].reshape(step * cols2, 4 * ch1)
                    for kf in range(3) for kr in range(3)
                ]
                acc = jnp.dot(
                    jnp.concatenate(taps, axis=1), w1[...].reshape(-1, 2 * ch1),
                    preferred_element_type=F32,
                ).reshape(step, cols2, 2 * ch1)
                acc = acc + resid[s, f, pl.ds(first, step)].astype(F32)
                row = first + lax.broadcasted_iota(jnp.int32, (step, 1, 1), 0)
                keep = (row < rows) | has_down
                acc = jnp.where(keep, acc, 0.0)
                stage_h[:, 0:cols2] = acc[:, :, 0:ch1]
                h3[pl.ds(first, step), :, 0 : 2 * ch1] = acc.astype(BF16)
                h3[pl.ds(first, step), :, 2 * ch1 : 3 * ch1] = stage_h[:, 1 : cols2 + 1].astype(BF16)
                return inner

            lax.fori_loop(0, chunks, chunk, 0)
            taps = [
                jnp.concatenate([h3[2 * i + p] for i in range(rows2)], axis=0) for p in range(3)
            ]
            value = jnp.dot(
                jnp.concatenate(taps, axis=1), wd[...].reshape(-1, ch2), preferred_element_type=F32
            ).astype(BF16).reshape(rows2, cols2, ch2)
            red[f, s] = value
            gbuf[f, s, 1 : rows2 + 1] = silu(value.astype(F32)).astype(BF16)
            return carry

        lax.fori_loop(0, slots, slot, 0)

    def spread_gated(source, s, e):
        v = source
        wide = v.astype(F32)
        stage_g[:, 8 : cols2 + 8] = wide
        g3[s, e, :, :, ch2 : 2 * ch2] = v
        g3[s, e, :, :, 0:ch2] = stage_g[:, 7 : cols2 + 7].astype(BF16)
        g3[s, e, :, :, 2 * ch2 : 3 * ch2] = stage_g[:, 9 : cols2 + 9].astype(BF16)

    def spread_gated_own(f):
        def slot(s, carry):
            spread_gated(gbuf[f, s], s, f + 2)
            return carry

        lax.fori_loop(0, slots, slot, 0)

    def spread_gated_arrived(e):
        @pl.when(has_prev)
        def _():
            def slot(s, carry):
                spread_gated(garr[e][pairing[0, s]], s, e)
                return carry

            lax.fori_loop(0, slots, slot, 0)

        @pl.when(jnp.logical_not(has_prev))
        def _():
            g3[:, e] = jnp.zeros((slots, rows2 + 2, cols2, 3 * ch2), BF16)

    stores = [
        pltpu.make_async_copy(obuf.at[f], out.at[:, f], local_sem.at[5 + f]) for f in range(frames)
    ]

    def second_section(f):
        def slot(s, carry):
            taps = [
                g3[s, f + kf, kr : kr + rows2].reshape(rows2 * cols2, 3 * ch2)
                for kf in range(3) for kr in range(3)
            ]
            acc = jnp.dot(
                jnp.concatenate(taps, axis=1), w2[...].reshape(-1, ch2), preferred_element_type=F32
            ).reshape(rows2, cols2, ch2)
            obuf[f, s] = (red[f, s].astype(F32) + acc).astype(BF16)
            return carry

        lax.fori_loop(0, slots, slot, 0)
        stores[f].start()

    def arrive_and_relay(move, row_moves):
        arrive(move)
        for item in row_moves:
            start(item)

    loads[0].wait()
    for item in own_rows:
        arrive(item)
    for f in range(frames):
        spread_own(f)
    for load in loads[1:4]:
        load.wait()
    for f in range(frames - 1, 1, -1):
        first_section(f)
        for item in gated_rows[f]:
            start(item)
        if f >= frames - 2:
            start(gated_moves[f - frames + 2])
    arrive_and_relay(frame_moves[1], frame_rows[1])
    for f in range(frames - 1, 1, -1):
        for item in gated_rows[f]:
            arrive(item)
        spread_gated_own(f)
    for item in frame_rows[1]:
        arrive(item)
    spread_arrived(1)
    first_section(1)
    for item in gated_rows[1]:
        start(item)
    loads[4].wait()
    for f in range(frames - 1, 3, -1):
        second_section(f)
    for item in gated_rows[1]:
        arrive(item)
    spread_gated_own(1)
    second_section(3)
    arrive_and_relay(frame_moves[0], frame_rows[0])
    for item in frame_rows[0]:
        arrive(item)
    spread_arrived(0)
    first_section(0)
    for item in gated_rows[0]:
        start(item)
    arrive_and_relay(gated_moves[1], gated_frame_rows[1])
    for item in gated_rows[0]:
        arrive(item)
    spread_gated_own(0)
    second_section(2)
    for item in gated_frame_rows[1]:
        arrive(item)
    spread_gated_arrived(1)
    second_section(1)
    arrive_and_relay(gated_moves[0], gated_frame_rows[0])
    for item in gated_frame_rows[0]:
        arrive(item)
    spread_gated_arrived(0)
    second_section(0)
    for copy, sends in sent:
        @pl.when(sends)
        def _():
            copy.wait_send()
    for store in stores:
        store.wait()


def on_device(n_tm, n_dom, video_group, pairing, weight_one, weight_down, weight_two):
    slots, frames, rows, width, ch1 = video_group.shape
    ch2 = weight_two.shape[-1]
    rows2, cols2 = rows // 2, width // 2
    step = chunk_rows(rows + 1, cols2, 512)
    any_spec = pl.BlockSpec(memory_space=pl.ANY)
    copies = 2 + 2 + 4 + 2 + 2 * frames + 4
    return pl.pallas_call(
        functools.partial(kernel, n_tm, n_dom),
        out_shape=jax.ShapeDtypeStruct((slots, frames, rows2, cols2, ch2), BF16),
        in_specs=[any_spec, pl.BlockSpec(memory_space=pltpu.SMEM), any_spec, any_spec, any_spec],
        out_specs=any_spec,
        scratch_shapes=[
            pltpu.VMEM((slots, frames, rows + 3, width, ch1), BF16),
            pltpu.VMEM((slots, rows + 3, width, ch1), BF16),
            pltpu.VMEM((slots, rows + 3, width, ch1), BF16),
            pltpu.VMEM((slots, frames + 2, rows + 3, cols2, 4 * ch1), BF16),
            pltpu.VMEM((slots, frames, rows + 1, cols2, 2 * ch1), BF16),
            pltpu.VMEM((9, 4 * ch1, 2 * ch1), BF16),
            pltpu.VMEM((3, 3 * ch1, ch2), BF16),
            pltpu.VMEM((9, 3 * ch2, ch2), BF16),
            pltpu.VMEM((rows + 3, width + 16, ch1), F32),
            pltpu.VMEM((rows + 1, width, ch1), F32),
            pltpu.VMEM((rows + 1, cols2, 3 * ch1), BF16),
            pltpu.VMEM((step, cols2 + 8, ch1), F32),
            pltpu.VMEM((frames, slots, rows2, cols2, ch2), BF16),
            pltpu.VMEM((frames, slots, rows2 + 2, cols2, ch2), BF16),
            pltpu.VMEM((slots, rows2 + 2, cols2, ch2), BF16),
            pltpu.VMEM((slots, rows2 + 2, cols2, ch2), BF16),
            pltpu.VMEM((slots, frames + 2, rows2 + 2, cols2, 3 * ch2), BF16),
            pltpu.VMEM((rows2 + 2, cols2 + 16, ch2), F32),
            pltpu.VMEM((frames, slots, rows2, cols2, ch2), BF16),
            pltpu.SemaphoreType.DMA((5 + frames,)),
            pltpu.SemaphoreType.DMA((copies,)),
            pltpu.SemaphoreType.DMA((copies,)),
        ],
        compiler_params=pltpu.CompilerParams(
            collective_id=0, has_side_effects=True, vmem_limit_bytes=63 * 1024 * 1024
        ),
        name="block",
    )(
        video_group,
        pairing,
        weight_one.reshape(9, 3 * ch1, ch1),
        weight_down.reshape(3, 3 * ch1, ch2),
        weight_two.reshape(9, 3 * ch2, ch2),
    )


def solution(mesh):
    return jax.shard_map(
        functools.partial(on_device, mesh.shape["tm"], mesh.shape["dom"]),
        mesh=mesh,
        in_specs=(P(None, "tm", "dom", None, None), P("tm", None), P(), P(), P()),
        out_specs=P(None, "tm", "dom", None, None),
        check_vma=False,
    )
```

profile of v0, /device:TPU:19, one launch (start us, length us, event | category | flops | bytes accessed | tf_op | source)
XLA Modules:
  0.0 84.5 jit_solution(6601513742831972494)
XLA Ops:
  0.0 81.5 %block.1 = bf16[2,4,7,64,256]{4,3,2,1,0:T(8,128)(2,1)} custom-call(bf16[2,4,14,128,128]{4,3,2,1,0:T(8,128)(2,1)} %video.1, s32[1,2]{1,0:T(1,128)} %pairing.1, bf16[9,384,128]{2,1,0:T(8,128)(2,1)} %bitcast.4, bf16[3,384,256]{2,1,0:T(8,128)(2,1)} %bitcast.5, bf16[9,768,256]{2,1,0:T(8,128)(2,1)} %bitcast.3), custom_call_target="tpu_custom_call" | custom-call | tf_op jit(solution)/shard_map/block/pallas_call | solution.py:344
  81.6 2.9 %copy.7 = bf16[2,4,7,64,256]{4,3,2,1,0:T(8,128)(2,1)} copy(bf16[2,4,7,64,256]{4,3,2,1,0:T(8,128)(2,1)} %block.1) | data formatting | bytes 3670016
where the time goes:
time: 84.6 us; the launch traced here: 84.5 us
  Pallas kernels  81.5 us (96%)
  local copies, waits for them, and re-layouts  2.94 us (3%)
    pallas_call x1, Pallas kernels, on_device(): pl.pallas_call(functools.partial(kernel, n_tm, n_dom), out_shape=jax.Shap...  81.5 us
    unnamed x1, local copies, waits for them, and re-layouts  2.94 us

commit v1 on v0

v1 whole, which is shorter than its diff:
```python
import functools

import jax
import jax.numpy as jnp
from jax import lax
from jax.experimental import pallas as pl
from jax.experimental.pallas import tpu as pltpu
from jax.sharding import PartitionSpec as P

MESH = pl.DeviceIdType.MESH
F32, BF16 = jnp.float32, jnp.bfloat16


def silu(v):
    half = 0.5 * v
    return half + half * jnp.tanh(half)


def chunk_rows(rows, width, limit):
    return max(d for d in range(1, rows + 1) if rows % d == 0 and (d == 1 or d * width <= limit))


def kernel(
    n_tm, n_dom,
    video, pairing, weight_one, weight_down, weight_two, out,
    vbuf, x4, resid, w1, wd, w2, stage, stage_raw, h3, stage_h,
    red, gbuf, g3, stage_g, obuf, oacc, pbuf, parr0, parr1, qbuf, qarr0, qarr1,
    local_sem, send_sem, recv_sem,
):
    slots, frames, rows, width, ch1 = video.shape
    rows2, cols2, ch2 = rows // 2, width // 2, out.shape[-1]
    tm, dom = lax.axis_index("tm"), lax.axis_index("dom")
    parr, qarr = (parr0, parr1), (qarr0, qarr1)
    has_prev, has_next = tm > 0, tm < n_tm - 1
    has_up, has_down = dom > 0, dom < n_dom - 1
    prev, nxt, up, down = (tm - 1, dom), (tm + 1, dom), (tm, dom - 1), (tm, dom + 1)

    loads = [
        pltpu.make_async_copy(video, vbuf.at[:, :, 1 : rows + 1], local_sem.at[0]),
        pltpu.make_async_copy(weight_one, w1.at[:, 0 : 3 * ch1, 0:ch1], local_sem.at[1]),
        pltpu.make_async_copy(weight_one, w1.at[:, ch1 : 4 * ch1, ch1 : 2 * ch1], local_sem.at[2]),
        pltpu.make_async_copy(weight_down, wd, local_sem.at[3]),
        pltpu.make_async_copy(weight_two, w2, local_sem.at[4]),
    ]
    for load in loads:
        load.start()

    barrier = pltpu.get_barrier_semaphore()
    for there, device in ((has_prev, prev), (has_next, nxt), (has_up, up), (has_down, down)):
        @pl.when(there)
        def _():
            pl.semaphore_signal(barrier, inc=1, device_id=device, device_id_type=MESH)
    peers = sum(there.astype(jnp.int32) for there in (has_prev, has_next, has_up, has_down))
    pl.semaphore_wait(barrier, peers)

    sent = []

    def remote(src, dst, device, sends, receives):
        index = len(sent)
        copy = pltpu.make_async_remote_copy(
            src_ref=src, dst_ref=dst, send_sem=send_sem.at[index], recv_sem=recv_sem.at[index],
            device_id=device, device_id_type=MESH,
        )
        sent.append((copy, sends))
        return copy, sends, receives

    def start(item):
        @pl.when(item[1])
        def _():
            item[0].start()

    def arrive(item):
        @pl.when(item[2])
        def _():
            item[0].wait_recv()

    own_rows = [
        remote(video.at[:, :, 0:2], vbuf.at[:, :, rows + 1 : rows + 3], up, has_up, has_down),
        remote(video.at[:, :, rows - 1 : rows], vbuf.at[:, :, 0:1], down, has_down, has_up),
    ]
    gated_rows = [
        [
            remote(gbuf.at[f, :, 1:2], gbuf.at[f, :, rows2 + 1 : rows2 + 2], up, has_up, has_down),
            remote(gbuf.at[f, :, rows2 : rows2 + 1], gbuf.at[f, :, 0:1], down, has_down, has_up),
        ]
        for f in range(frames)
    ]
    first_moves = [remote(pbuf.at[e], parr[e], nxt, has_next, has_prev) for e in (0, 1)]
    second_moves = [remote(qbuf.at[e], qarr[e], nxt, has_next, has_prev) for e in (0, 1)]

    for item in own_rows:
        start(item)

    w1[:, 3 * ch1 : 4 * ch1, 0:ch1] = jnp.zeros((w1.shape[0], ch1, ch1), BF16)
    w1[:, 0:ch1, ch1 : 2 * ch1] = jnp.zeros((w1.shape[0], ch1, ch1), BF16)
    stage[:, 0:8] = jnp.zeros((rows + 3, 8, ch1), F32)
    stage[:, width + 8 : width + 16] = jnp.zeros((rows + 3, 8, ch1), F32)
    stage_h[:, cols2 : cols2 + 8] = jnp.zeros((stage_h.shape[0], 8, ch1), F32)
    stage_g[:, 0:8] = jnp.zeros((rows2 + 2, 8, ch2), F32)
    stage_g[:, cols2 + 8 : cols2 + 16] = jnp.zeros((rows2 + 2, 8, ch2), F32)

    @pl.when(jnp.logical_not(has_up))
    def _():
        vbuf[:, :, 0:1] = jnp.zeros((slots, frames, 1, width, ch1), BF16)
        gbuf[:, :, 0:1] = jnp.zeros((frames, slots, 1, cols2, ch2), BF16)

    @pl.when(jnp.logical_not(has_down))
    def _():
        vbuf[:, :, rows + 1 : rows + 3] = jnp.zeros((slots, frames, 2, width, ch1), BF16)
        gbuf[:, :, rows2 + 1 : rows2 + 2] = jnp.zeros((frames, slots, 1, cols2, ch2), BF16)

    @pl.when(jnp.logical_not(has_prev))
    def _():
        for e in (0, 1):
            parr[e][...] = jnp.zeros(parr[e].shape, BF16)
            qarr[e][...] = jnp.zeros(qarr[e].shape, BF16)

    def each_slot(body):
        def slot(s, carry):
            body(s)
            return carry

        lax.fori_loop(0, slots, slot, 0)

    def spread_own(f):
        def slot(s):
            def activated(r, inner):
                stage[r, 8 : width + 8] = silu(vbuf[s, f, r].astype(F32))
                for c in range(4):
                    part = stage[r, pl.ds(7 + c, cols2, stride=2), :]
                    x4[s, f, r, :, c * ch1 : (c + 1) * ch1] = part.astype(BF16)
                return inner

            lax.fori_loop(0, rows + 3, activated, 0, unroll=2)

            def raw(r, inner):
                stage_raw[r] = vbuf[s, f, r + 1].astype(F32)
                for c in range(2):
                    part = stage_raw[r, pl.ds(c, cols2, stride=2), :]
                    resid[s, f, r, :, c * ch1 : (c + 1) * ch1] = part.astype(BF16)
                return inner

            lax.fori_loop(0, rows + 1, raw, 0, unroll=2)

        each_slot(slot)

    step = chunk_rows(rows + 1, cols2, 512)
    chunks = (rows + 1) // step

    def reduced_of(s, first_tap, sources, skip):
        def chunk(i, inner):
            first = i * step
            taps = [
                x4[s, f, pl.ds(first + kr, step)].reshape(step * cols2, 4 * ch1)
                for f in sources for kr in range(3)
            ]
            weight = w1[3 * first_tap : 3 * (first_tap + len(sources))].reshape(-1, 2 * ch1)
            acc = jnp.dot(
                jnp.concatenate(taps, axis=1), weight, preferred_element_type=F32
            ).reshape(step, cols2, 2 * ch1)
            if skip is not None:
                acc = acc + resid[s, skip, pl.ds(first, step)].astype(F32)
            row = first + lax.broadcasted_iota(jnp.int32, (step, 1, 1), 0)
            acc = jnp.where((row < rows) | has_down, acc, 0.0)
            stage_h[:, 0:cols2] = acc[:, :, 0:ch1]
            h3[pl.ds(first, step), :, 0 : 2 * ch1] = acc.astype(BF16)
            h3[pl.ds(first, step), :, 2 * ch1 : 3 * ch1] = stage_h[:, 1 : cols2 + 1].astype(BF16)
            return inner

        lax.fori_loop(0, chunks, chunk, 0)
        taps = [
            jnp.concatenate([h3[2 * i + p] for i in range(rows2)], axis=0) for p in range(3)
        ]
        return jnp.dot(
            jnp.concatenate(taps, axis=1), wd[...].reshape(-1, ch2), preferred_element_type=F32
        ).reshape(rows2, cols2, ch2)

    def first_section(f):
        first_tap = max(0, 2 - f)
        sources = range(f + first_tap - 2, f + 1)
        if f < 2:
            arrive(first_moves[f])

        def slot(s):
            value = reduced_of(s, first_tap, sources, f)
            if f < 2:
                value = value + parr[f][pairing[0, s]].astype(F32)
            value = value.astype(BF16)
            red[f, s] = value
            gbuf[f, s, 1 : rows2 + 1] = silu(value.astype(F32)).astype(BF16)

        each_slot(slot)
        for item in gated_rows[f]:
            start(item)

    def first_partial(e):
        @pl.when(has_next)
        def _():
            def slot(s):
                value = reduced_of(s, 0, range(frames + e - 2, frames), None)
                pbuf[e, s] = value.astype(BF16)

            each_slot(slot)

        start(first_moves[e])

    def spread_gated(f):
        for item in gated_rows[f]:
            arrive(item)

        def slot(s):
            v = gbuf[f, s]
            stage_g[:, 8 : cols2 + 8] = v.astype(F32)
            g3[s, f, :, :, ch2 : 2 * ch2] = v
            g3[s, f, :, :, 0:ch2] = stage_g[:, 7 : cols2 + 7].astype(BF16)
            g3[s, f, :, :, 2 * ch2 : 3 * ch2] = stage_g[:, 9 : cols2 + 9].astype(BF16)

        each_slot(slot)

    def convolved(s, first_tap, sources):
        taps = [
            g3[s, f, kr : kr + rows2].reshape(rows2 * cols2, 3 * ch2)
            for f in sources for kr in range(3)
        ]
        weight = w2[3 * first_tap : 3 * (first_tap + len(sources))].reshape(-1, ch2)
        return jnp.dot(
            jnp.concatenate(taps, axis=1), weight, preferred_element_type=F32
        ).reshape(rows2, cols2, ch2)

    stores = [
        pltpu.make_async_copy(obuf.at[f], out.at[:, f], local_sem.at[5 + f]) for f in range(frames)
    ]

    def second_section(f):
        first_tap = max(0, 2 - f)
        sources = range(f + first_tap - 2, f + 1)

        def slot(s):
            value = red[f, s].astype(F32) + convolved(s, first_tap, sources)
            if f < 2:
                oacc[f, s] = value
            else:
                obuf[f, s] = value.astype(BF16)

        each_slot(slot)
        if f >= 2:
            stores[f].start()

    def second_partial(e):
        @pl.when(has_next)
        def _():
            def slot(s):
                qbuf[e, s] = convolved(s, 0, range(frames + e - 2, frames)).astype(BF16)

            each_slot(slot)

        start(second_moves[e])

    def finish(f):
        arrive(second_moves[f])

        def slot(s):
            obuf[f, s] = (oacc[f, s] + qarr[f][pairing[0, s]].astype(F32)).astype(BF16)

        each_slot(slot)
        stores[f].start()

    loads[0].wait()
    for item in own_rows:
        arrive(item)
    spread_own(frames - 1)
    for load in loads[1:4]:
        load.wait()
    first_partial(1)
    spread_own(frames - 2)
    first_partial(0)
    for f in range(frames - 2):
        spread_own(f)
    first_section(frames - 1)
    first_section(frames - 2)
    loads[4].wait()
    spread_gated(frames - 1)
    second_partial(1)
    spread_gated(frames - 2)
    second_partial(0)
    for f in range(frames - 3, -1, -1):
        first_section(f)
    for f in range(frames - 3, 0, -1):
        spread_gated(f)
    for f in range(frames - 1, 2, -1):
        second_section(f)
    spread_gated(0)
    for f in range(2, -1, -1):
        second_section(f)
    finish(1)
    finish(0)
    for copy, sends in sent:
        @pl.when(sends)
        def _():
            copy.wait_send()
    for store in stores:
        store.wait()


def on_device(n_tm, n_dom, video_group, pairing, weight_one, weight_down, weight_two):
    slots, frames, rows, width, ch1 = video_group.shape
    ch2 = weight_two.shape[-1]
    rows2, cols2 = rows // 2, width // 2
    step = chunk_rows(rows + 1, cols2, 512)
    any_spec = pl.BlockSpec(memory_space=pl.ANY)
    copies = 2 + 2 * frames + 4
    return pl.pallas_call(
        functools.partial(kernel, n_tm, n_dom),
        out_shape=jax.ShapeDtypeStruct((slots, frames, rows2, cols2, ch2), BF16),
        in_specs=[any_spec, pl.BlockSpec(memory_space=pltpu.SMEM), any_spec, any_spec, any_spec],
        out_specs=any_spec,
        scratch_shapes=[
            pltpu.VMEM((slots, frames, rows + 3, width, ch1), BF16),
            pltpu.VMEM((slots, frames, rows + 3, cols2, 4 * ch1), BF16),
            pltpu.VMEM((slots, frames, rows + 1, cols2, 2 * ch1), BF16),
            pltpu.VMEM((9, 4 * ch1, 2 * ch1), BF16),
            pltpu.VMEM((3, 3 * ch1, ch2), BF16),
            pltpu.VMEM((9, 3 * ch2, ch2), BF16),
            pltpu.VMEM((rows + 3, width + 16, ch1), F32),
            pltpu.VMEM((rows + 1, width, ch1), F32),
            pltpu.VMEM((rows + 1, cols2, 3 * ch1), BF16),
            pltpu.VMEM((step, cols2 + 8, ch1), F32),
            pltpu.VMEM((frames, slots, rows2, cols2, ch2), BF16),
            pltpu.VMEM((frames, slots, rows2 + 2, cols2, ch2), BF16),
            pltpu.VMEM((slots, frames, rows2 + 2, cols2, 3 * ch2), BF16),
            pltpu.VMEM((rows2 + 2, cols2 + 16, ch2), F32),
            pltpu.VMEM((frames, slots, rows2, cols2, ch2), BF16),
            pltpu.VMEM((2, slots, rows2, cols2, ch2), F32),
            pltpu.VMEM((2, slots, rows2, cols2, ch2), BF16),
            pltpu.VMEM((slots, rows2, cols2, ch2), BF16),
            pltpu.VMEM((slots, rows2, cols2, ch2), BF16),
            pltpu.VMEM((2, slots, rows2, cols2, ch2), BF16),
            pltpu.VMEM((slots, rows2, cols2, ch2), BF16),
            pltpu.VMEM((slots, rows2, cols2, ch2), BF16),
            pltpu.SemaphoreType.DMA((5 + frames,)),
            pltpu.SemaphoreType.DMA((copies,)),
            pltpu.SemaphoreType.DMA((copies,)),
        ],
        compiler_params=pltpu.CompilerParams(
            collective_id=0, has_side_effects=True, vmem_limit_bytes=63 * 1024 * 1024
        ),
        name="block",
    )(
        video_group,
        pairing,
        weight_one.reshape(9, 3 * ch1, ch1),
        weight_down.reshape(3, 3 * ch1, ch2),
        weight_two.reshape(9, 3 * ch2, ch2),
    )


def solution(mesh):
    return jax.shard_map(
        functools.partial(on_device, mesh.shape["tm"], mesh.shape["dom"]),
        mesh=mesh,
        in_specs=(P(None, "tm", "dom", None, None), P("tm", None), P(), P(), P()),
        out_specs=P(None, "tm", "dom", None, None),
        check_vma=False,
    )
```

time: 84.6 us -> 71.8 us (0.85)
  Pallas kernels: 81.5 us -> 68.7 us
    pallas_call x1, Pallas kernels: 81.5 us -> 68.7 us  [on_device(): pl.pallas_call(functools.partial(kernel, n_tm, n_dom), out_shape=jax.Shap...]
where the time goes in v1:
time: 71.8 us; the launch traced here: 71.7 us
  Pallas kernels  68.7 us (96%)
  local copies, waits for them, and re-layouts  2.94 us (4%)
    pallas_call x1, Pallas kernels, on_device(): pl.pallas_call(functools.partial(kernel, n_tm, n_dom), out_shape=jax.Shap...  68.7 us
    unnamed x1, local copies, waits for them, and re-layouts  2.94 us

profile of v1, /device:TPU:19, one launch (start us, length us, event | category | flops | bytes accessed | tf_op | source)
XLA Modules:
  0.0 71.7 jit_solution(15370164761489581793)
XLA Ops:
  0.0 68.7 %block.1 = bf16[2,4,7,64,256]{4,3,2,1,0:T(8,128)(2,1)} custom-call(bf16[2,4,14,128,128]{4,3,2,1,0:T(8,128)(2,1)} %video.1, s32[1,2]{1,0:T(1,128)} %pairing.1, bf16[9,384,128]{2,1,0:T(8,128)(2,1)} %bitcast.4, bf16[3,384,256]{2,1,0:T(8,128)(2,1)} %bitcast.5, bf16[9,768,256]{2,1,0:T(8,128)(2,1)} %bitcast.3), custom_call_target="tpu_custom_call" | custom-call | tf_op jit(solution)/shard_map/block/pallas_call | solution.py:312
  68.8 2.9 %copy.7 = bf16[2,4,7,64,256]{4,3,2,1,0:T(8,128)(2,1)} copy(bf16[2,4,7,64,256]{4,3,2,1,0:T(8,128)(2,1)} %block.1) | data formatting | bytes 3670016
